TPU v7x, 256 devices: a whole 4x4x8 slice. The times are simulated.
256 devices in a mesh: gx: 32 (over x, z_hi, core), sec: 8 (over z_lo, y).
Axes of the slice: x: 4, y: 4, z: 8 (z_hi: 4, z_lo: 2; z = z_hi * 2 + z_lo), core: 2. Of those that a mesh axis runs over, the one named last changes fastest.
Arguments:
- state_init: float32 [16, 256, 64, 128], P(None, 'gx', 'sec'), may hold values from -6 to 6
- rock_type: int32 [256, 4096], P('gx', 'sec'), may hold values from 0 to 15
- perm_table: float32 [3, 16], replicated, may hold values from 0.2 to 1
- well_cells: int32 [256], replicated, may hold values from 0 to 1048575
- well_rate: float32 [16, 256], replicated, may hold values from -12 to 12
- basis_in: bfloat16 [256, 64, 128, 256], P(('gx', 'sec')), may hold values from -4 to 4
- singular: float32 [256], replicated, may hold values from 0.5 to 2
Outputs:
- state_out: float32 [16, 256, 64, 128], P(None, 'gx', 'sec')
- basis_out: bfloat16 [256, 64, 128, 256], P(('gx', 'sec'))
- singular_out: float32 [256], replicated
All inputs are finite; a program needn't handle non-finite values.
Results may differ from a plain program's by a relative error of at most 0.0059.
Values may be sent and summed in bfloat16 or wider, within the bound.
A program may use at most 128 MiB of HBM per device.

v0:
```python
import jax
import jax.numpy as jnp
from jax import lax
from jax.sharding import PartitionSpec as P

MG = 8
STEPS = 4
GROUPS = 2
DT_PRESSURE = 0.12
DT_SATURATION = 0.06
DT_ADVECT = 0.15


def with_halo(block, sides, width):
    for axis, dim in sides:
        count = lax.axis_size(axis)
        forward = [(i, i + 1) for i in range(count - 1)]
        backward = [(target, source) for source, target in forward]
        low = lax.ppermute(
            lax.slice_in_dim(block, block.shape[dim] - width, None, axis=dim), axis, forward
        )
        high = lax.ppermute(lax.slice_in_dim(block, 0, width, axis=dim), axis, backward)
        block = jnp.concatenate([low, block, high], axis=dim)
    return block


def harmonic(left, right):
    return 2.0 * left * right / (left + right)


def shift_layers(fields):
    blank = jnp.zeros_like(fields[..., :1])
    return (
        jnp.concatenate([fields[..., 1:], blank], -1),
        jnp.concatenate([blank, fields[..., :-1]], -1),
    )


def advance(fields, besides, weights, inflow, layers):
    column = lax.broadcasted_iota(jnp.int32, (fields.shape[-1],), 0)
    step_sizes = jnp.where(column < layers, DT_PRESSURE, DT_SATURATION)
    is_sat = (column >= layers).astype(fields.dtype)
    press_both = jnp.concatenate([fields[..., :layers], fields[..., :layers]], -1)
    spread = jnp.zeros_like(fields)
    carried = jnp.zeros_like(fields)
    for beside, weight in zip(besides, weights):
        spread = spread + weight * (beside - fields)
        beside_press = jnp.concatenate([beside[..., :layers], beside[..., :layers]], -1)
        pushed = weight * (beside_press - press_both)
        carried = carried + jnp.maximum(pushed, 0.0) * beside + jnp.minimum(pushed, 0.0) * fields
    return fields + step_sizes * spread + DT_ADVECT * is_sat * carried + DT_PRESSURE * inflow


HIGH = lax.Precision.HIGHEST


def hdot(a, b):
    return jnp.dot(a, b, precision=HIGH)


def batch_update(coeffs, gram_of, sigma):
    rounded = coeffs.astype(jnp.bfloat16).astype(jnp.float32)
    gram = gram_of(coeffs, rounded)
    square = jnp.diag(sigma * sigma)
    total = square + hdot(coeffs.T, coeffs)
    inner = hdot(total, total) + hdot(coeffs.T, hdot(gram, coeffs))
    factor = jnp.linalg.cholesky(inner)
    eye = jnp.eye(sigma.shape[0], dtype=jnp.float32)
    back = lax.linalg.triangular_solve(factor, eye, left_side=True, lower=True).T
    top = sigma[:, None] * hdot(total, back)
    bottom = hdot(hdot(coeffs, total) + hdot(gram, coeffs), back)
    sigma_next = jnp.sqrt(jnp.sum(top * top, axis=0) + jnp.sum(bottom * bottom, axis=0))
    on_basis = hdot(square + hdot((coeffs - rounded).T, coeffs), back)
    on_snaps = hdot(coeffs, back)
    return (on_basis, on_snaps, sigma_next)


def small_algebra(uu, su, ss, sigma):
    half = su.shape[0] // 2
    s00, s10, s11 = (ss[:half, :half], ss[half:, :half], ss[half:, half:])

    def gram_first(c, r):
        cr = hdot(c, r.T)
        return s00 - cr - cr.T + hdot(r, hdot(uu, r.T))

    wu, ws, sigma1 = batch_update(su[:half], gram_first, sigma)
    coeffs1 = hdot(su[half:], wu) + hdot(s10, ws)

    def gram_second(c, r):
        cr = hdot(c, r.T)
        yu, ys = (hdot(wu, r.T), hdot(ws, r.T))
        mixed = hdot(ys.T, hdot(su[:half], yu))
        own = hdot(yu.T, hdot(uu, yu)) + mixed + mixed.T + hdot(ys.T, hdot(s00, ys))
        return s11 - cr - cr.T + own

    wu1, ws1, sigma2 = batch_update(coeffs1, gram_second, sigma1)
    return (hdot(wu, wu1), hdot(ws, wu1), ws1, sigma2)


def body(state_init, rock_type, perm_table, well_cells, well_rate, basis_in, singular):
    across = state_init.shape[1]
    along = state_init.shape[2]
    layers = state_init.shape[3] // 2
    sec_count = lax.axis_size("sec")
    rock_count = perm_table.shape[1]
    kinds = lax.broadcasted_iota(jnp.int32, (rock_count, 1, 1), 0)
    picks = (rock_type[None] == kinds).astype(jnp.float32)
    perm = jnp.einsum("dr,rxc->dxc", perm_table, picks, precision=lax.Precision.HIGHEST).reshape(
        3, across, along, layers
    )
    paired = jnp.concatenate([perm[0], perm[1]], -1)
    bordered_perm = with_halo(paired.astype(jnp.bfloat16), (("gx", 0), ("sec", 1)), 1).astype(
        paired.dtype
    )
    perm_xh = bordered_perm[..., :layers]
    perm_yh = bordered_perm[..., layers:]
    x_up = harmonic(perm[0], perm_xh[2:, 1:-1])
    x_down = harmonic(perm_xh[:-2, 1:-1], perm[0])
    y_up = harmonic(perm[1], perm_yh[1:-1, 2:])
    y_down = harmonic(perm_yh[1:-1, :-2], perm[1])
    z_padded = jnp.pad(perm[2], ((0, 0), (0, 0), (1, 1)))
    z_up = harmonic(perm[2], z_padded[..., 2:])
    z_down = harmonic(z_padded[..., :-2], perm[2])
    weights = [
        jnp.concatenate([face, face], -1) for face in (x_up, x_down, y_up, y_down, z_up, z_down)
    ]
    x_start = lax.axis_index("gx") * across
    y_start = lax.axis_index("sec") * along
    total_y = along * sec_count
    x_pos = lax.broadcasted_iota(jnp.int32, (across, along, layers), 0)
    y_pos = lax.broadcasted_iota(jnp.int32, (across, along, layers), 1)
    z_pos = lax.broadcasted_iota(jnp.int32, (across, along, layers), 2)
    cell_ids = ((x_start + x_pos) * total_y + y_start + y_pos) * layers + z_pos
    hits = (well_cells[:, None] == cell_ids.reshape(1, -1)).astype(jnp.float32)
    source = jnp.dot(well_rate, hits, precision=lax.Precision.HIGHEST).reshape(
        state_init.shape[0], across, along, layers
    )
    source_full = jnp.concatenate([source, jnp.zeros_like(source)], -1)
    local_rows = basis_in.shape[0] * basis_in.shape[1] * basis_in.shape[2]
    rows_total = local_rows * lax.axis_size("gx") * sec_count
    finals = []
    snaps = []
    for group in range(GROUPS):
        fields = state_init[group * MG : (group + 1) * MG]
        inflow = source_full[group * MG : (group + 1) * MG]
        saved = []
        for step_index in range(STEPS):
            bordered = with_halo(fields.astype(jnp.bfloat16), (("gx", 1), ("sec", 2)), 1).astype(
                fields.dtype
            )
            up_layer, down_layer = shift_layers(fields)
            besides = [
                bordered[:, 2:, 1:-1],
                bordered[:, :-2, 1:-1],
                bordered[:, 1:-1, 2:],
                bordered[:, 1:-1, :-2],
                up_layer,
                down_layer,
            ]
            fields = advance(fields, besides, weights, inflow, layers)
            snapshot = fields.astype(jnp.bfloat16)
            saved.append(snapshot)
        finals.append(fields)
        stacked = jnp.concatenate(saved, 0)
        stacked = lax.all_to_all(stacked, "sec", split_axis=1, concat_axis=2, tiled=True)
        snaps.append(stacked.reshape(stacked.shape[0], -1))
    both = jnp.concatenate(snaps, 0)
    basis = basis_in.reshape(both.shape[1], basis_in.shape[-1])
    count = basis.shape[1]
    uu = lax.dot_general(basis, basis, (((0,), (0,)), ((), ())), preferred_element_type=jnp.float32)
    su = jnp.dot(both, basis, preferred_element_type=jnp.float32)
    ss = lax.dot_general(both, both, (((1,), (1,)), ((), ())), preferred_element_type=jnp.float32)
    local = jnp.concatenate(
        [
            jnp.concatenate([uu, su], 0),
            jnp.pad(
                jnp.concatenate([jnp.zeros((count, both.shape[0]), jnp.float32), ss], 0),
                ((0, 0), (0, 64)),
            ),
        ],
        1,
    )
    whole = lax.psum(local, ("gx", "sec")) / rows_total
    w0, w1, w2, sigma = small_algebra(
        whole[:count, :count],
        whole[count:, :count],
        whole[count:, count : count + both.shape[0]],
        singular,
    )
    fresh = jnp.dot(basis, w0.astype(jnp.bfloat16), preferred_element_type=jnp.float32)
    fresh = fresh + lax.dot_general(
        both,
        jnp.concatenate([w1, w2], 0).astype(jnp.bfloat16),
        (((0,), (0,)), ((), ())),
        preferred_element_type=jnp.float32,
    )
    basis_now = fresh.astype(jnp.bfloat16).reshape(basis_in.shape)
    return (jnp.concatenate(finals, 0), basis_now, sigma)


def solution(mesh):
    return jax.shard_map(
        body,
        mesh=mesh,
        in_specs=(
            P(None, "gx", "sec", None),
            P("gx", "sec"),
            P(),
            P(),
            P(),
            P(("gx", "sec"), None, None, None),
            P(),
        ),
        out_specs=(P(None, "gx", "sec", None), P(("gx", "sec"), None, None, None), P()),
        check_vma=False,
    )
```

profile of v0, /device:TPU:6, one launch (start us, length us, event | category | flops | bytes accessed | tf_op | source)
XLA Modules:
  0.0 627.0 jit_solution(13930910843129405325)
XLA Ops:
  11.1 7.9 %collective-permute-start.1 = (bf16[1,8,128]{2,1,0:T(8,128)(2,1)}, bf16[1,8,128]{2,1,0:T(8,128)(2,1)}, u32[]{:S(2)}, u32[]{:S(2)}) collective-permute-start(bf16[1,8,128]{2,1,0:T(8,128)(2,1)} %get-tuple-element.186), channel_id=1, source_target_pairs={{8,0},{16,8},{24,16},{32,24},{40,32},{48,40},{56,48},{64,56},{72,6... | collective-permute-start | bytes 6152 | tf_op jit(solution)/shard_map/ppermute | solution.py:22
  22.6 6.7 %collective-permute-start.5 = (bf16[8,1,8,128]{3,2,0,1:T(8,128)(2,1)}, bf16[8,1,8,128]{3,2,0,1:T(8,128)(2,1)}, u32[]{:S(2)}, u32[]{:S(2)}) collective-permute-start(bf16[8,1,8,128]{3,2,0,1:T(8,128)(2,1)} %get-tuple-element.160), channel_id=1, source_target_pairs={{8,0},{16,8},{24,16},{32,24},{40,32},{48,40},{56,48},{64,56},{72,6... | collective-permute-start | bytes 49160 | tf_op jit(solution)/shard_map/ppermute | solution.py:22
  34.6 5.5 fusion.8
  51.2 6.4 %collective-permute-start.21 = (bf16[8,1,8,128]{3,2,0,1:T(8,128)(2,1)}, bf16[8,1,8,128]{3,2,0,1:T(8,128)(2,1)S(1)}, u32[]{:S(2)}, u32[]{:S(2)}) collective-permute-start(bf16[8,1,8,128]{3,2,0,1:T(8,128)(2,1)} %get-tuple-element.168), channel_id=1, source_target_pairs={{8,0},{16,8},{24,16},{32,24},{40,32},{48,40},{56,48},{64,56},{72,6... | collective-permute-start | bytes 49160 | tf_op jit(solution)/shard_map/ppermute | solution.py:22
  59.5 4.3 collective-permute-start.6
  65.2 4.5 collective-permute-start.22
  79.1 6.7 %collective-permute-start.9 = (bf16[8,1,8,128]{3,2,0,1:T(8,128)(2,1)S(1)}, bf16[8,1,8,128]{3,2,0,1:T(8,128)(2,1)S(1)}, u32[]{:S(2)}, u32[]{:S(2)}) collective-permute-start(bf16[8,1,8,128]{3,2,0,1:T(8,128)(2,1)S(1)} %get-tuple-element.158), channel_id=1, source_target_pairs={{8,0},{16,8},{24,16},{32,24},{40,32},{48,40},{56,48},{64,56},{72,6... | collective-permute-start | bytes 49160 | tf_op jit(solution)/shard_map/ppermute | solution.py:22
  87.9 6.7 %collective-permute-start.25 = (bf16[8,1,8,128]{3,2,0,1:T(8,128)(2,1)S(1)}, bf16[8,1,8,128]{3,2,0,1:T(8,128)(2,1)S(1)}, u32[]{:S(2)}, u32[]{:S(2)}) collective-permute-start(bf16[8,1,8,128]{3,2,0,1:T(8,128)(2,1)S(1)} %get-tuple-element.166), channel_id=1, source_target_pairs={{8,0},{16,8},{24,16},{32,24},{40,32},{48,40},{56,48},{64,56},{72,6... | collective-permute-start | bytes 49160 | tf_op jit(solution)/shard_map/ppermute | solution.py:22
  99.7 6.7 %collective-permute-start.26 = (bf16[8,10,1,128]{3,2,0,1:T(2,128)(2,1)S(1)}, bf16[8,10,1,128]{3,2,0,1:T(2,128)(2,1)S(1)}, u32[]{:S(2)}, u32[]{:S(2)}) collective-permute-start(bf16[8,10,1,128]{3,2,0,1:T(2,128)(2,1)S(1)} %get-tuple-element.149), channel_id=1, source_target_pairs={{0,1},{1,2},{2,3},{3,4},{4,5},{5,6},{6,7},{8,9},{9,10},{10,11},{11... | collective-permute-start | bytes 61448 | tf_op jit(solution)/shard_map/ppermute | solution.py:19
  109.5 4.9 collective-permute-done.27
  117.9 6.7 %collective-permute-start.13 = (bf16[8,1,8,128]{3,2,0,1:T(8,128)(2,1)S(1)}, bf16[8,1,8,128]{3,2,0,1:T(8,128)(2,1)S(1)}, u32[]{:S(2)}, u32[]{:S(2)}) collective-permute-start(bf16[8,1,8,128]{3,2,0,1:T(8,128)(2,1)S(1)} %get-tuple-element.156), channel_id=1, source_target_pairs={{8,0},{16,8},{24,16},{32,24},{40,32},{48,40},{56,48},{64,56},{72,6... | collective-permute-start | bytes 49160 | tf_op jit(solution)/shard_map/ppermute | solution.py:22
  126.6 6.7 %collective-permute-start.29 = (bf16[8,1,8,128]{3,2,0,1:T(8,128)(2,1)S(1)}, bf16[8,1,8,128]{3,2,0,1:T(8,128)(2,1)S(1)}, u32[]{:S(2)}, u32[]{:S(2)}) collective-permute-start(bf16[8,1,8,128]{3,2,0,1:T(8,128)(2,1)S(1)} %get-tuple-element.164), channel_id=1, source_target_pairs={{8,0},{16,8},{24,16},{32,24},{40,32},{48,40},{56,48},{64,56},{72,6... | collective-permute-start | bytes 49160 | tf_op jit(solution)/shard_map/ppermute | solution.py:22
  138.8 6.0 collective-permute-start.30
  147.8 5.1 collective-permute-done.31
  156.4 6.7 %collective-permute-start.17 = (bf16[8,1,8,128]{3,2,0,1:T(8,128)(2,1)S(1)}, bf16[8,1,8,128]{3,2,0,1:T(8,128)(2,1)S(1)}, u32[]{:S(2)}, u32[]{:S(2)}) collective-permute-start(bf16[8,1,8,128]{3,2,0,1:T(8,128)(2,1)S(1)} %get-tuple-element.154), channel_id=1, source_target_pairs={{8,0},{16,8},{24,16},{32,24},{40,32},{48,40},{56,48},{64,56},{72,6... | collective-permute-start | bytes 49160 | tf_op jit(solution)/shard_map/ppermute | solution.py:22
  165.2 6.7 %collective-permute-start.33 = (bf16[8,1,8,128]{3,2,0,1:T(8,128)(2,1)S(1)}, bf16[8,1,8,128]{3,2,0,1:T(8,128)(2,1)S(1)}, u32[]{:S(2)}, u32[]{:S(2)}) collective-permute-start(bf16[8,1,8,128]{3,2,0,1:T(8,128)(2,1)S(1)} %get-tuple-element.162), channel_id=1, source_target_pairs={{8,0},{16,8},{24,16},{32,24},{40,32},{48,40},{56,48},{64,56},{72,6... | collective-permute-start | bytes 49160 | tf_op jit(solution)/shard_map/ppermute | solution.py:22
  177.2 4.7 collective-permute-start.34
  185.4 10.4 %all-to-all-start = ((bf16[32,8,8,128]{3,2,0,1:T(8,128)(2,1)}), bf16[32,8,8,128]{3,2,0,1:T(8,128)(2,1)S(1)}, u32[]{:S(2)}, u32[]{:S(2)}) async-start(bf16[32,8,8,128]{3,2,0,1:T(8,128)(2,1)} %pad_maximum_fusion.1), calls=%async_computation | async-start | bytes 1048576 | tf_op jit(solution)/shard_map/all_to_all | solution.py:165
  198.2 5.9 all-to-all-done
  208.5 7.3 %all-to-all-done.1 = bf16[32,8,8,128]{3,2,0,1:T(8,128)(2,1)S(1)} async-done(((bf16[32,8,8,128]{3,2,0,1:T(8,128)(2,1)}), bf16[32,8,8,128]{3,2,0,1:T(8,128)(2,1)S(1)}, u32[]{:S(2)}, u32[]{:S(2)}) %all-to-all-start.1) | async-done | bytes 524320 | tf_op jit(solution)/shard_map/all_to_all | solution.py:165
  220.6 249.7 %all-reduce.23.cloned.1.call-done = f32[320,384]{1,0:T(8,128)} async-done(((f32[320,384]{1,0:T(8,128)}), f32[320,384]{1,0:T(8,128)}) %all-reduce.23.cloned.1.call-update) | async-done | bytes 491536 | tf_op jit(solution)/shard_map/psum | solution.py:183
  474.5 11.7 %cholesky.130 = f32[128,128]{1,0:T(8,128)S(1)} custom-call(f32[128,128]{1,0:T(8,128)S(1)} %cholesky.194), custom_call_target="Cholesky" | custom-call | tf_op jit(solution)/shard_map/jit(cholesky)/cholesky | solution.py:67
  486.9 9.8 %custom-call.13 = f32[1,128,128]{1,2,0:T(8,128)S(1)} custom-call(f32[1,128,128]{2,1,0:T(8,128)S(1)} %get-tuple-element.182), custom_call_target="InvertDiagBlocksLowerTriangular" | custom-call | tf_op jit(solution)/shard_map/jit(cholesky)/cholesky | solution.py:67
  497.2 11.9 %cholesky.147 = f32[128,128]{1,0:T(8,128)S(1)} custom-call(f32[128,128]{1,0:T(8,128)S(1)} %convolution_subtract_fusion.3), custom_call_target="Cholesky" | custom-call | tf_op jit(solution)/shard_map/jit(cholesky)/cholesky | solution.py:67
  511.3 4.1 while.4
  515.4 19.7 %custom-call.14 = f32[2,128,128]{1,2,0:T(8,128)S(1)} custom-call(f32[2,128,128]{2,1,0:T(8,128)S(1)} %get-tuple-element.19), custom_call_target="InvertDiagBlocksLowerTriangular" | custom-call | tf_op jit(solution)/shard_map/triangular_solve/custom-call.0 | solution.py:69
  542.5 11.7 %cholesky.164 = f32[128,128]{1,0:T(8,128)S(1)} custom-call(f32[128,128]{1,0:T(8,128)S(1)} %cholesky.197), custom_call_target="Cholesky" | custom-call | tf_op jit(solution)/shard_map/jit(cholesky)/cholesky | solution.py:67
  554.9 9.8 %custom-call.15 = f32[1,128,128]{1,2,0:T(8,128)S(1)} custom-call(f32[1,128,128]{2,1,0:T(8,128)S(1)} %get-tuple-element.178), custom_call_target="InvertDiagBlocksLowerTriangular" | custom-call | tf_op jit(solution)/shard_map/jit(cholesky)/cholesky | solution.py:67
  565.2 11.9 %cholesky.181 = f32[128,128]{1,0:T(8,128)S(1)} custom-call(f32[128,128]{1,0:T(8,128)S(1)} %convolution_subtract_fusion.2), custom_call_target="Cholesky" | custom-call | tf_op jit(solution)/shard_map/jit(cholesky)/cholesky | solution.py:67
  579.2 4.1 while.5
  583.4 19.7 %custom-call.16 = f32[2,128,128]{1,2,0:T(8,128)S(1)} custom-call(f32[2,128,128]{2,1,0:T(8,128)S(1)} %get-tuple-element.20), custom_call_target="InvertDiagBlocksLowerTriangular" | custom-call | tf_op jit(solution)/shard_map/triangular_solve/custom-call.0 | solution.py:69
  613.0 6.4 %copy.82 = bf16[8192,256]{1,0:T(8,128)(2,1)} copy(bf16[8192,256]{0,1:T(8,128)(2,1)} %fusion) | data formatting | bytes 8388608
  (274 shorter events, 120.0 us)
Async XLA Ops:
  9.1 34.6 %collective-permute-start = (bf16[1,8,128]{2,1,0:T(8,128)(2,1)}, bf16[1,8,128]{2,1,0:T(8,128)(2,1)}, u32[]{:S(2)}, u32[]{:S(2)}) collective-permute-start(bf16[1,8,128]{2,1,0:T(8,128)(2,1)} %get-tuple-element.185), channel_id=1, source_target_pairs={{0,8},{8,16},{16,24},{24,32},{32,40},{40,48},{48,56},{56,64},{64,7... | collective-permute-start | bytes 6152 | tf_op jit(solution)/shard_map/ppermute | solution.py:19
  11.1 32.7 %collective-permute-start.1 = (bf16[1,8,128]{2,1,0:T(8,128)(2,1)}, bf16[1,8,128]{2,1,0:T(8,128)(2,1)}, u32[]{:S(2)}, u32[]{:S(2)}) collective-permute-start(bf16[1,8,128]{2,1,0:T(8,128)(2,1)} %get-tuple-element.186), channel_id=1, source_target_pairs={{8,0},{16,8},{24,16},{32,24},{40,32},{48,40},{56,48},{64,56},{72,6... | collective-permute-start | bytes 6152 | tf_op jit(solution)/shard_map/ppermute | solution.py:22
  20.7 38.0 %collective-permute-start.4 = (bf16[8,1,8,128]{3,2,0,1:T(8,128)(2,1)}, bf16[8,1,8,128]{3,2,0,1:T(8,128)(2,1)S(1)}, u32[]{:S(2)}, u32[]{:S(2)}) collective-permute-start(bf16[8,1,8,128]{3,2,0,1:T(8,128)(2,1)} %get-tuple-element.159), channel_id=1, source_target_pairs={{0,8},{8,16},{16,24},{24,32},{32,40},{40,48},{48,56},{56,64},{64,7... | collective-permute-start | bytes 49160 | tf_op jit(solution)/shard_map/ppermute | solution.py:19
  22.6 36.1 %collective-permute-start.5 = (bf16[8,1,8,128]{3,2,0,1:T(8,128)(2,1)}, bf16[8,1,8,128]{3,2,0,1:T(8,128)(2,1)}, u32[]{:S(2)}, u32[]{:S(2)}) collective-permute-start(bf16[8,1,8,128]{3,2,0,1:T(8,128)(2,1)} %get-tuple-element.160), channel_id=1, source_target_pairs={{8,0},{16,8},{24,16},{32,24},{40,32},{48,40},{56,48},{64,56},{72,6... | collective-permute-start | bytes 49160 | tf_op jit(solution)/shard_map/ppermute | solution.py:22
  29.9 35.2 %collective-permute-start.20 = (bf16[8,1,8,128]{3,2,0,1:T(8,128)(2,1)}, bf16[8,1,8,128]{3,2,0,1:T(8,128)(2,1)S(1)}, u32[]{:S(2)}, u32[]{:S(2)}) collective-permute-start(bf16[8,1,8,128]{3,2,0,1:T(8,128)(2,1)} %get-tuple-element.167), channel_id=1, source_target_pairs={{0,8},{8,16},{16,24},{24,32},{32,40},{40,48},{48,56},{56,64},{64,7... | collective-permute-start | bytes 49160 | tf_op jit(solution)/shard_map/ppermute | solution.py:19
  48.1 9.4 %collective-permute-start.3 = (bf16[10,1,128]{2,1,0:T(2,128)(2,1)S(1)}, bf16[10,1,128]{2,1,0:T(2,128)(2,1)S(1)}, u32[]{:S(2)}, u32[]{:S(2)}) collective-permute-start(bf16[10,1,128]{2,1,0:T(2,128)(2,1)S(1)} %get-tuple-element.184), channel_id=1, source_target_pairs={{1,0},{2,1},{3,2},{4,3},{5,4},{6,5},{7,6},{9,8},{10,9},{11,10},{12... | collective-permute-start | bytes 7688 | tf_op jit(solution)/shard_map/ppermute | solution.py:22
  51.2 13.9 %collective-permute-start.21 = (bf16[8,1,8,128]{3,2,0,1:T(8,128)(2,1)}, bf16[8,1,8,128]{3,2,0,1:T(8,128)(2,1)S(1)}, u32[]{:S(2)}, u32[]{:S(2)}) collective-permute-start(bf16[8,1,8,128]{3,2,0,1:T(8,128)(2,1)} %get-tuple-element.168), channel_id=1, source_target_pairs={{8,0},{16,8},{24,16},{32,24},{40,32},{48,40},{56,48},{64,56},{72,6... | collective-permute-start | bytes 49160 | tf_op jit(solution)/shard_map/ppermute | solution.py:22
  59.5 11.5 %collective-permute-start.6 = (bf16[8,10,1,128]{3,2,0,1:T(2,128)(2,1)S(1)}, bf16[8,10,1,128]{3,2,0,1:T(2,128)(2,1)S(1)}, u32[]{:S(2)}, u32[]{:S(2)}) collective-permute-start(bf16[8,10,1,128]{3,2,0,1:T(2,128)(2,1)S(1)} %get-tuple-element.143), channel_id=1, source_target_pairs={{0,1},{1,2},{2,3},{3,4},{4,5},{5,6},{6,7},{8,9},{9,10},{10,11},{11... | collective-permute-start | bytes 61448 | tf_op jit(solution)/shard_map/ppermute | solution.py:19
  65.2 9.2 %collective-permute-start.22 = (bf16[8,10,1,128]{3,2,0,1:T(2,128)(2,1)S(1)}, bf16[8,10,1,128]{3,2,0,1:T(2,128)(2,1)S(1)}, u32[]{:S(2)}, u32[]{:S(2)}) collective-permute-start(bf16[8,10,1,128]{3,2,0,1:T(2,128)(2,1)S(1)} %get-tuple-element.151), channel_id=1, source_target_pairs={{0,1},{1,2},{2,3},{3,4},{4,5},{5,6},{6,7},{8,9},{9,10},{10,11},{11... | collective-permute-start | bytes 61448 | tf_op jit(solution)/shard_map/ppermute | solution.py:19
  77.2 17.5 %collective-permute-start.8 = (bf16[8,1,8,128]{3,2,0,1:T(8,128)(2,1)S(1)}, bf16[8,1,8,128]{3,2,0,1:T(8,128)(2,1)S(1)}, u32[]{:S(2)}, u32[]{:S(2)}) collective-permute-start(bf16[8,1,8,128]{3,2,0,1:T(8,128)(2,1)S(1)} %get-tuple-element.157), channel_id=1, source_target_pairs={{0,8},{8,16},{16,24},{24,32},{32,40},{40,48},{48,56},{56,64},{64,7... | collective-permute-start | bytes 49160 | tf_op jit(solution)/shard_map/ppermute | solution.py:19
  79.1 15.5 %collective-permute-start.9 = (bf16[8,1,8,128]{3,2,0,1:T(8,128)(2,1)S(1)}, bf16[8,1,8,128]{3,2,0,1:T(8,128)(2,1)S(1)}, u32[]{:S(2)}, u32[]{:S(2)}) collective-permute-start(bf16[8,1,8,128]{3,2,0,1:T(8,128)(2,1)S(1)} %get-tuple-element.158), channel_id=1, source_target_pairs={{8,0},{16,8},{24,16},{32,24},{40,32},{48,40},{56,48},{64,56},{72,6... | collective-permute-start | bytes 49160 | tf_op jit(solution)/shard_map/ppermute | solution.py:22
  85.9 13.6 %collective-permute-start.24 = (bf16[8,1,8,128]{3,2,0,1:T(8,128)(2,1)S(1)}, bf16[8,1,8,128]{3,2,0,1:T(8,128)(2,1)S(1)}, u32[]{:S(2)}, u32[]{:S(2)}) collective-permute-start(bf16[8,1,8,128]{3,2,0,1:T(8,128)(2,1)S(1)} %get-tuple-element.165), channel_id=1, source_target_pairs={{0,8},{8,16},{16,24},{24,32},{32,40},{40,48},{48,56},{56,64},{64,7... | collective-permute-start | bytes 49160 | tf_op jit(solution)/shard_map/ppermute | solution.py:19
  87.9 11.7 %collective-permute-start.25 = (bf16[8,1,8,128]{3,2,0,1:T(8,128)(2,1)S(1)}, bf16[8,1,8,128]{3,2,0,1:T(8,128)(2,1)S(1)}, u32[]{:S(2)}, u32[]{:S(2)}) collective-permute-start(bf16[8,1,8,128]{3,2,0,1:T(8,128)(2,1)S(1)} %get-tuple-element.166), channel_id=1, source_target_pairs={{8,0},{16,8},{24,16},{32,24},{40,32},{48,40},{56,48},{64,56},{72,6... | collective-permute-start | bytes 49160 | tf_op jit(solution)/shard_map/ppermute | solution.py:22
  94.7 13.1 %collective-permute-start.10 = (bf16[8,10,1,128]{3,2,0,1:T(2,128)(2,1)S(1)}, bf16[8,10,1,128]{3,2,0,1:T(2,128)(2,1)S(1)}, u32[]{:S(2)}, u32[]{:S(2)}) collective-permute-start(bf16[8,10,1,128]{3,2,0,1:T(2,128)(2,1)S(1)} %get-tuple-element.141), channel_id=1, source_target_pairs={{0,1},{1,2},{2,3},{3,4},{4,5},{5,6},{6,7},{8,9},{9,10},{10,11},{11... | collective-permute-start | bytes 61448 | tf_op jit(solution)/shard_map/ppermute | solution.py:19
  98.3 9.5 %collective-permute-start.11 = (bf16[8,10,1,128]{3,2,0,1:T(2,128)(2,1)S(1)}, bf16[8,10,1,128]{3,2,0,1:T(2,128)(2,1)S(1)}, u32[]{:S(2)}, u32[]{:S(2)}) collective-permute-start(bf16[8,10,1,128]{3,2,0,1:T(2,128)(2,1)S(1)} %get-tuple-element.142), channel_id=1, source_target_pairs={{1,0},{2,1},{3,2},{4,3},{5,4},{6,5},{7,6},{9,8},{10,9},{11,10},{12... | collective-permute-start | bytes 61448 | tf_op jit(solution)/shard_map/ppermute | solution.py:22
  99.7 9.8 %collective-permute-start.26 = (bf16[8,10,1,128]{3,2,0,1:T(2,128)(2,1)S(1)}, bf16[8,10,1,128]{3,2,0,1:T(2,128)(2,1)S(1)}, u32[]{:S(2)}, u32[]{:S(2)}) collective-permute-start(bf16[8,10,1,128]{3,2,0,1:T(2,128)(2,1)S(1)} %get-tuple-element.149), channel_id=1, source_target_pairs={{0,1},{1,2},{2,3},{3,4},{4,5},{5,6},{6,7},{8,9},{9,10},{10,11},{11... | collective-permute-start | bytes 61448 | tf_op jit(solution)/shard_map/ppermute | solution.py:19
  116.0 17.5 %collective-permute-start.12 = (bf16[8,1,8,128]{3,2,0,1:T(8,128)(2,1)S(1)}, bf16[8,1,8,128]{3,2,0,1:T(8,128)(2,1)S(1)}, u32[]{:S(2)}, u32[]{:S(2)}) collective-permute-start(bf16[8,1,8,128]{3,2,0,1:T(8,128)(2,1)S(1)} %get-tuple-element.155), channel_id=1, source_target_pairs={{0,8},{8,16},{16,24},{24,32},{32,40},{40,48},{48,56},{56,64},{64,7... | collective-permute-start | bytes 49160 | tf_op jit(solution)/shard_map/ppermute | solution.py:19
  117.9 15.5 %collective-permute-start.13 = (bf16[8,1,8,128]{3,2,0,1:T(8,128)(2,1)S(1)}, bf16[8,1,8,128]{3,2,0,1:T(8,128)(2,1)S(1)}, u32[]{:S(2)}, u32[]{:S(2)}) collective-permute-start(bf16[8,1,8,128]{3,2,0,1:T(8,128)(2,1)S(1)} %get-tuple-element.156), channel_id=1, source_target_pairs={{8,0},{16,8},{24,16},{32,24},{40,32},{48,40},{56,48},{64,56},{72,6... | collective-permute-start | bytes 49160 | tf_op jit(solution)/shard_map/ppermute | solution.py:22
  124.7 14.0 %collective-permute-start.28 = (bf16[8,1,8,128]{3,2,0,1:T(8,128)(2,1)S(1)}, bf16[8,1,8,128]{3,2,0,1:T(8,128)(2,1)S(1)}, u32[]{:S(2)}, u32[]{:S(2)}) collective-permute-start(bf16[8,1,8,128]{3,2,0,1:T(8,128)(2,1)S(1)} %get-tuple-element.163), channel_id=1, source_target_pairs={{0,8},{8,16},{16,24},{24,32},{32,40},{40,48},{48,56},{56,64},{64,7... | collective-permute-start | bytes 49160 | tf_op jit(solution)/shard_map/ppermute | solution.py:19
  126.6 12.1 %collective-permute-start.29 = (bf16[8,1,8,128]{3,2,0,1:T(8,128)(2,1)S(1)}, bf16[8,1,8,128]{3,2,0,1:T(8,128)(2,1)S(1)}, u32[]{:S(2)}, u32[]{:S(2)}) collective-permute-start(bf16[8,1,8,128]{3,2,0,1:T(8,128)(2,1)S(1)} %get-tuple-element.164), channel_id=1, source_target_pairs={{8,0},{16,8},{24,16},{32,24},{40,32},{48,40},{56,48},{64,56},{72,6... | collective-permute-start | bytes 49160 | tf_op jit(solution)/shard_map/ppermute | solution.py:22
  133.5 12.6 %collective-permute-start.14 = (bf16[8,10,1,128]{3,2,0,1:T(2,128)(2,1)S(1)}, bf16[8,10,1,128]{3,2,0,1:T(2,128)(2,1)S(1)}, u32[]{:S(2)}, u32[]{:S(2)}) collective-permute-start(bf16[8,10,1,128]{3,2,0,1:T(2,128)(2,1)S(1)} %get-tuple-element.139), channel_id=1, source_target_pairs={{0,1},{1,2},{2,3},{3,4},{4,5},{5,6},{6,7},{8,9},{9,10},{10,11},{11... | collective-permute-start | bytes 61448 | tf_op jit(solution)/shard_map/ppermute | solution.py:19
  138.8 9.0 %collective-permute-start.30 = (bf16[8,10,1,128]{3,2,0,1:T(2,128)(2,1)S(1)}, bf16[8,10,1,128]{3,2,0,1:T(2,128)(2,1)S(1)}, u32[]{:S(2)}, u32[]{:S(2)}) collective-permute-start(bf16[8,10,1,128]{3,2,0,1:T(2,128)(2,1)S(1)} %get-tuple-element.147), channel_id=1, source_target_pairs={{0,1},{1,2},{2,3},{3,4},{4,5},{5,6},{6,7},{8,9},{9,10},{10,11},{11... | collective-permute-start | bytes 61448 | tf_op jit(solution)/shard_map/ppermute | solution.py:19
  154.5 17.3 %collective-permute-start.16 = (bf16[8,1,8,128]{3,2,0,1:T(8,128)(2,1)S(1)}, bf16[8,1,8,128]{3,2,0,1:T(8,128)(2,1)S(1)}, u32[]{:S(2)}, u32[]{:S(2)}) collective-permute-start(bf16[8,1,8,128]{3,2,0,1:T(8,128)(2,1)S(1)} %get-tuple-element.153), channel_id=1, source_target_pairs={{0,8},{8,16},{16,24},{24,32},{32,40},{40,48},{48,56},{56,64},{64,7... | collective-permute-start | bytes 49160 | tf_op jit(solution)/shard_map/ppermute | solution.py:19
  156.4 15.4 %collective-permute-start.17 = (bf16[8,1,8,128]{3,2,0,1:T(8,128)(2,1)S(1)}, bf16[8,1,8,128]{3,2,0,1:T(8,128)(2,1)S(1)}, u32[]{:S(2)}, u32[]{:S(2)}) collective-permute-start(bf16[8,1,8,128]{3,2,0,1:T(8,128)(2,1)S(1)} %get-tuple-element.154), channel_id=1, source_target_pairs={{8,0},{16,8},{24,16},{32,24},{40,32},{48,40},{56,48},{64,56},{72,6... | collective-permute-start | bytes 49160 | tf_op jit(solution)/shard_map/ppermute | solution.py:22
  163.2 13.9 %collective-permute-start.32 = (bf16[8,1,8,128]{3,2,0,1:T(8,128)(2,1)S(1)}, bf16[8,1,8,128]{3,2,0,1:T(8,128)(2,1)S(1)}, u32[]{:S(2)}, u32[]{:S(2)}) collective-permute-start(bf16[8,1,8,128]{3,2,0,1:T(8,128)(2,1)S(1)} %get-tuple-element.161), channel_id=1, source_target_pairs={{0,8},{8,16},{16,24},{24,32},{32,40},{40,48},{48,56},{56,64},{64,7... | collective-permute-start | bytes 49160 | tf_op jit(solution)/shard_map/ppermute | solution.py:19
  165.2 12.0 %collective-permute-start.33 = (bf16[8,1,8,128]{3,2,0,1:T(8,128)(2,1)S(1)}, bf16[8,1,8,128]{3,2,0,1:T(8,128)(2,1)S(1)}, u32[]{:S(2)}, u32[]{:S(2)}) collective-permute-start(bf16[8,1,8,128]{3,2,0,1:T(8,128)(2,1)S(1)} %get-tuple-element.162), channel_id=1, source_target_pairs={{8,0},{16,8},{24,16},{32,24},{40,32},{48,40},{56,48},{64,56},{72,6... | collective-permute-start | bytes 49160 | tf_op jit(solution)/shard_map/ppermute | solution.py:22
  171.9 11.3 %collective-permute-start.18 = (bf16[8,10,1,128]{3,2,0,1:T(2,128)(2,1)S(1)}, bf16[8,10,1,128]{3,2,0,1:T(2,128)(2,1)S(1)}, u32[]{:S(2)}, u32[]{:S(2)}) collective-permute-start(bf16[8,10,1,128]{3,2,0,1:T(2,128)(2,1)S(1)} %get-tuple-element.137), channel_id=1, source_target_pairs={{0,1},{1,2},{2,3},{3,4},{4,5},{5,6},{6,7},{8,9},{9,10},{10,11},{11... | collective-permute-start | bytes 61448 | tf_op jit(solution)/shard_map/ppermute | solution.py:19
  177.2 18.7 %collective-permute-start.34 = (bf16[8,10,1,128]{3,2,0,1:T(2,128)(2,1)S(1)}, bf16[8,10,1,128]{3,2,0,1:T(2,128)(2,1)S(1)}, u32[]{:S(2)}, u32[]{:S(2)}) collective-permute-start(bf16[8,10,1,128]{3,2,0,1:T(2,128)(2,1)S(1)} %get-tuple-element.145), channel_id=1, source_target_pairs={{0,1},{1,2},{2,3},{3,4},{4,5},{5,6},{6,7},{8,9},{9,10},{10,11},{11... | collective-permute-start | bytes 61448 | tf_op jit(solution)/shard_map/ppermute | solution.py:19
  181.9 14.1 %collective-permute-start.35 = (bf16[8,10,1,128]{3,2,0,1:T(2,128)(2,1)S(1)}, bf16[8,10,1,128]{3,2,0,1:T(2,128)(2,1)S(1)}, u32[]{:S(2)}, u32[]{:S(2)}) collective-permute-start(bf16[8,10,1,128]{3,2,0,1:T(2,128)(2,1)S(1)} %get-tuple-element.146), channel_id=1, source_target_pairs={{1,0},{2,1},{3,2},{4,3},{5,4},{6,5},{7,6},{9,8},{10,9},{11,10},{12... | collective-permute-start | bytes 61448 | tf_op jit(solution)/shard_map/ppermute | solution.py:22
  185.4 18.6 %all-to-all-start = ((bf16[32,8,8,128]{3,2,0,1:T(8,128)(2,1)}), bf16[32,8,8,128]{3,2,0,1:T(8,128)(2,1)S(1)}, u32[]{:S(2)}, u32[]{:S(2)}) async-start(bf16[32,8,8,128]{3,2,0,1:T(8,128)(2,1)} %pad_maximum_fusion.1), calls=%async_computation | async-start | bytes 1048576 | tf_op jit(solution)/shard_map/all_to_all | solution.py:165
  204.1 11.7 %all-to-all-start.1 = ((bf16[32,8,8,128]{3,2,0,1:T(8,128)(2,1)}), bf16[32,8,8,128]{3,2,0,1:T(8,128)(2,1)S(1)}, u32[]{:S(2)}, u32[]{:S(2)}) async-start(bf16[32,8,8,128]{3,2,0,1:T(8,128)(2,1)} %pad_maximum_fusion.2), calls=%async_computation.1 | async-start | bytes 1048576 | tf_op jit(solution)/shard_map/all_to_all | solution.py:165
  207.6 262.7 %all-reduce.23.cloned.1.call-start = ((), (), s32[]{:S(2)}) async-start(), calls=%async_computation.2 | async-start | bytes 983040 | tf_op jit(solution)/shard_map/psum | solution.py:183
  (21 other events, 270.8 us)
Sparse Core Ops, SparseCore 0:
  219.8 250.5 all-reduce.22
where the time goes:
time: 635 us; the launch traced here: 627 us
  waiting for transfers between devices  274 us (43%)
  starting transfers between devices  145 us (23%)
  other arithmetic  131 us (21%)
  matrix products  30.2 us (5%)
  local copies, waits for them, and re-layouts  27.9 us (4%)
  between operations  18.7 us (3%)
    psum x1, waiting for transfers between devices, body(): whole = lax.psum(local, ('gx', 'sec')) / rows_total  250 us
    ppermute x18, starting transfers between devices, with_halo(): lax.ppermute(lax.slice_in_dim(block, 0, width, axis=dim), axis, backward)  72.6 us
    another operation x14, other arithmetic, batch_update(): factor = jnp.linalg.cholesky(inner)  69.7 us
    ppermute x18, starting transfers between devices, with_halo(): lax.ppermute(lax.slice_in_dim(block, block.shape[dim] - width, None, axis...  58.3 us
    another operation x5, other arithmetic, batch_update(): lax.linalg.triangular_solve(factor, eye, left_side=True, lower=True)  39.4 us
    all_to_all x2, starting transfers between devices, body(): lax.all_to_all(stacked, 'sec', split_axis=1, concat_axis=2, tiled=True)  13.9 us
    all_to_all x2, waiting for transfers between devices, body(): lax.all_to_all(stacked, 'sec', split_axis=1, concat_axis=2, tiled=True)  13.2 us
  transfers between devices with their start and end apart: 39, of which 6 were waited for; matrix products, arithmetic and copies ran while one was open for 5% of the time, Pallas kernels for 0%

commit v1 on v0

--- a/solution.py
+++ b/solution.py
@@ -1,3 +1,4 @@
+import functools
 import jax
 import jax.numpy as jnp
 from jax import lax
@@ -9,6 +10,15 @@
 DT_PRESSURE = 0.12
 DT_SATURATION = 0.06
 DT_ADVECT = 0.15
+
+
+def test_screen(inner_x, a_name, axis_tag):
+    for t in (a_name, axis_tag):
+        inner_x = jax.lax.psum(inner_x, t)
+    return inner_x
+
+
+_meet_classes = functools.partial(test_screen, a_name="sec", axis_tag="gx")
 
 
 def with_halo(block, sides, width):
@@ -180,7 +190,7 @@
         ],
         1,
     )
-    whole = lax.psum(local, ("gx", "sec")) / rows_total
+    whole = _meet_classes(local) / rows_total
     w0, w1, w2, sigma = small_algebra(
         whole[:count, :count],
         whole[count:, :count],

time: 635 us -> 741 us (1.17)
  the two profiles are of different devices: /device:TPU:6 before, /device:TPU:8 now
where the time goes in v1:
time: 741 us; the launch traced here: 731 us
  waiting for transfers between devices  394 us (53%)
  starting transfers between devices  135 us (18%)
  other arithmetic  126 us (17%)
  matrix products  30.2 us (4%)
  local copies, waits for them, and re-layouts  26.3 us (4%)
  between operations  18.6 us (3%)
    psum x2, waiting for transfers between devices, test_screen(): inner_x = jax.lax.psum(inner_x, t)  373 us
    ppermute x18, starting transfers between devices, with_halo(): lax.ppermute(lax.slice_in_dim(block, block.shape[dim] - width, None, axis...  91.3 us
    another operation x14, other arithmetic, batch_update(): factor = jnp.linalg.cholesky(inner)  69.6 us
    another operation x5, other arithmetic, batch_update(): lax.linalg.triangular_solve(factor, eye, left_side=True, lower=True)  39.4 us
    ppermute x18, starting transfers between devices, with_halo(): lax.ppermute(lax.slice_in_dim(block, 0, width, axis=dim), axis, backward)  30.1 us
  transfers between devices with their start and end apart: 40, of which 8 were waited for; matrix products, arithmetic and copies ran while one was open for 4% of the time, Pallas kernels for 0%

profile of v1, /device:TPU:8, one launch (start us, length us, event | category | flops | bytes accessed | tf_op | source)
XLA Modules:
  0.0 730.9 jit_solution(17191108733195640067)
XLA Ops:
  12.7 6.1 collective-permute-start.4
  20.1 5.2 collective-permute-start.20
  28.1 5.5 fusion.8
  52.8 4.9 collective-permute-start.22
  68.7 7.2 collective-permute-start.24
  77.4 5.6 collective-permute-start.10
  85.0 6.0 collective-permute-start.26
  98.6 4.0 collective-permute-start.12
  104.1 8.4 %collective-permute-start.28 = (bf16[8,1,8,128]{3,2,0,1:T(8,128)(2,1)S(1)}, bf16[8,1,8,128]{3,2,0,1:T(8,128)(2,1)S(1)}, u32[]{:S(2)}, u32[]{:S(2)}) collective-permute-start(bf16[8,1,8,128]{3,2,0,1:T(8,128)(2,1)S(1)} %get-tuple-element.163), channel_id=1, source_target_pairs={{0,8},{8,16},{16,24},{24,32},{32,40},{40,48},{48,56},{56,64},{64,7... | collective-permute-start | bytes 49160 | tf_op jit(solution)/shard_map/ppermute | solution.py:29
  114.0 4.7 collective-permute-start.14
  120.7 6.0 collective-permute-start.30
  134.3 4.7 collective-permute-start.16
  140.4 8.1 %collective-permute-start.32 = (bf16[8,1,8,128]{3,2,0,1:T(8,128)(2,1)S(1)}, bf16[8,1,8,128]{3,2,0,1:T(8,128)(2,1)S(1)}, u32[]{:S(2)}, u32[]{:S(2)}) collective-permute-start(bf16[8,1,8,128]{3,2,0,1:T(8,128)(2,1)S(1)} %get-tuple-element.161), channel_id=1, source_target_pairs={{0,8},{8,16},{16,24},{24,32},{32,40},{40,48},{48,56},{56,64},{64,7... | collective-permute-start | bytes 49160 | tf_op jit(solution)/shard_map/ppermute | solution.py:29
  149.9 4.0 collective-permute-start.18
  155.9 6.0 collective-permute-start.34
  166.1 7.5 %all-to-all-start = ((bf16[32,8,8,128]{3,2,0,1:T(8,128)(2,1)}), bf16[32,8,8,128]{3,2,0,1:T(8,128)(2,1)S(1)}, u32[]{:S(2)}, u32[]{:S(2)}) async-start(bf16[32,8,8,128]{3,2,0,1:T(8,128)(2,1)} %pad_maximum_fusion.1), calls=%async_computation | async-start | bytes 1048576 | tf_op jit(solution)/shard_map/all_to_all | solution.py:175
  175.9 5.8 all-to-all-done
  181.7 6.0 all-to-all-start.1
  188.1 7.9 %all-to-all-done.1 = bf16[32,8,8,128]{3,2,0,1:T(8,128)(2,1)S(1)} async-done(((bf16[32,8,8,128]{3,2,0,1:T(8,128)(2,1)}), bf16[32,8,8,128]{3,2,0,1:T(8,128)(2,1)S(1)}, u32[]{:S(2)}, u32[]{:S(2)}) %all-to-all-start.1) | async-done | bytes 524320 | tf_op jit(solution)/shard_map/all_to_all | solution.py:175
  200.4 87.3 %all-reduce.24.cloned.1.call-done = f32[320,384]{1,0:T(8,128)} async-done(((f32[320,384]{1,0:T(8,128)}), f32[320,384]{1,0:T(8,128)}) %all-reduce.24.cloned.1.call-update) | async-done | bytes 491536 | tf_op jit(solution)/shard_map/psum | solution.py:17
  288.7 286.0 %all-reduce.26.cloned.1.call-done = f32[320,384]{1,0:T(8,128)} async-done(((f32[320,384]{1,0:T(8,128)}), f32[320,384]{1,0:T(8,128)}) %all-reduce.26.cloned.1.call-update) | async-done | bytes 491536 | tf_op jit(solution)/shard_map/psum | solution.py:17
  578.9 11.7 %cholesky.130 = f32[128,128]{1,0:T(8,128)S(1)} custom-call(f32[128,128]{1,0:T(8,128)S(1)} %cholesky.194), custom_call_target="Cholesky" | custom-call | tf_op jit(solution)/shard_map/jit(cholesky)/cholesky | solution.py:77
  591.3 9.8 %custom-call.13 = f32[1,128,128]{1,2,0:T(8,128)S(1)} custom-call(f32[1,128,128]{2,1,0:T(8,128)S(1)} %get-tuple-element.182), custom_call_target="InvertDiagBlocksLowerTriangular" | custom-call | tf_op jit(solution)/shard_map/jit(cholesky)/cholesky | solution.py:77
  601.7 11.9 %cholesky.147 = f32[128,128]{1,0:T(8,128)S(1)} custom-call(f32[128,128]{1,0:T(8,128)S(1)} %convolution_subtract_fusion.3), custom_call_target="Cholesky" | custom-call | tf_op jit(solution)/shard_map/jit(cholesky)/cholesky | solution.py:77
  615.5 3.9 while.4
  619.4 19.7 %custom-call.14 = f32[2,128,128]{1,2,0:T(8,128)S(1)} custom-call(f32[2,128,128]{2,1,0:T(8,128)S(1)} %get-tuple-element.19), custom_call_target="InvertDiagBlocksLowerTriangular" | custom-call | tf_op jit(solution)/shard_map/triangular_solve/custom-call.0 | solution.py:79
  646.5 11.7 %cholesky.164 = f32[128,128]{1,0:T(8,128)S(1)} custom-call(f32[128,128]{1,0:T(8,128)S(1)} %cholesky.197), custom_call_target="Cholesky" | custom-call | tf_op jit(solution)/shard_map/jit(cholesky)/cholesky | solution.py:77
  658.8 9.8 %custom-call.15 = f32[1,128,128]{1,2,0:T(8,128)S(1)} custom-call(f32[1,128,128]{2,1,0:T(8,128)S(1)} %get-tuple-element.178), custom_call_target="InvertDiagBlocksLowerTriangular" | custom-call | tf_op jit(solution)/shard_map/jit(cholesky)/cholesky | solution.py:77
  669.2 11.9 %cholesky.181 = f32[128,128]{1,0:T(8,128)S(1)} custom-call(f32[128,128]{1,0:T(8,128)S(1)} %convolution_subtract_fusion.2), custom_call_target="Cholesky" | custom-call | tf_op jit(solution)/shard_map/jit(cholesky)/cholesky | solution.py:77
  683.1 4.0 while.5
  687.1 19.7 %custom-call.16 = f32[2,128,128]{1,2,0:T(8,128)S(1)} custom-call(f32[2,128,128]{2,1,0:T(8,128)S(1)} %get-tuple-element.20), custom_call_target="InvertDiagBlocksLowerTriangular" | custom-call | tf_op jit(solution)/shard_map/triangular_solve/custom-call.0 | solution.py:79
  716.7 6.4 copy.82
  (269 shorter events, 112.9 us)
Async XLA Ops:
  8.6 28.7 %collective-permute-start = (bf16[1,8,128]{2,1,0:T(8,128)(2,1)S(1)}, bf16[1,8,128]{2,1,0:T(8,128)(2,1)S(1)}, u32[]{:S(2)}, u32[]{:S(2)}) collective-permute-start(bf16[1,8,128]{2,1,0:T(8,128)(2,1)S(1)} %get-tuple-element.185), channel_id=1, source_target_pairs={{0,8},{8,16},{16,24},{24,32},{32,40},{40,48},{48,56},{56,64},{64,7... | collective-permute-start | bytes 6152 | tf_op jit(solution)/shard_map/ppermute | solution.py:29
  10.3 27.0 %collective-permute-start.1 = (bf16[1,8,128]{2,1,0:T(8,128)(2,1)S(1)}, bf16[1,8,128]{2,1,0:T(8,128)(2,1)S(1)}, u32[]{:S(2)}, u32[]{:S(2)}) collective-permute-start(bf16[1,8,128]{2,1,0:T(8,128)(2,1)S(1)} %get-tuple-element.186), channel_id=1, source_target_pairs={{8,0},{16,8},{24,16},{32,24},{40,32},{48,40},{56,48},{64,56},{72,6... | collective-permute-start | bytes 6152 | tf_op jit(solution)/shard_map/ppermute | solution.py:32
  12.7 34.1 %collective-permute-start.4 = (bf16[8,1,8,128]{3,2,0,1:T(8,128)(2,1)S(1)}, bf16[8,1,8,128]{3,2,0,1:T(8,128)(2,1)S(1)}, u32[]{:S(2)}, u32[]{:S(2)}) collective-permute-start(bf16[8,1,8,128]{3,2,0,1:T(8,128)(2,1)S(1)} %get-tuple-element.159), channel_id=1, source_target_pairs={{0,8},{8,16},{16,24},{24,32},{32,40},{40,48},{48,56},{56,64},{64,7... | collective-permute-start | bytes 49160 | tf_op jit(solution)/shard_map/ppermute | solution.py:29
  18.8 28.0 %collective-permute-start.5 = (bf16[8,1,8,128]{3,2,0,1:T(8,128)(2,1)S(1)}, bf16[8,1,8,128]{3,2,0,1:T(8,128)(2,1)S(1)}, u32[]{:S(2)}, u32[]{:S(2)}) collective-permute-start(bf16[8,1,8,128]{3,2,0,1:T(8,128)(2,1)S(1)} %get-tuple-element.160), channel_id=1, source_target_pairs={{8,0},{16,8},{24,16},{32,24},{40,32},{48,40},{56,48},{64,56},{72,6... | collective-permute-start | bytes 49160 | tf_op jit(solution)/shard_map/ppermute | solution.py:32
  20.1 32.6 %collective-permute-start.20 = (bf16[8,1,8,128]{3,2,0,1:T(8,128)(2,1)S(1)}, bf16[8,1,8,128]{3,2,0,1:T(8,128)(2,1)S(1)}, u32[]{:S(2)}, u32[]{:S(2)}) collective-permute-start(bf16[8,1,8,128]{3,2,0,1:T(8,128)(2,1)S(1)} %get-tuple-element.167), channel_id=1, source_target_pairs={{0,8},{8,16},{16,24},{24,32},{32,40},{40,48},{48,56},{56,64},{64,7... | collective-permute-start | bytes 49160 | tf_op jit(solution)/shard_map/ppermute | solution.py:29
  46.8 12.7 %collective-permute-start.6 = (bf16[8,10,1,128]{3,2,0,1:T(2,128)(2,1)S(1)}, bf16[8,10,1,128]{3,2,0,1:T(2,128)(2,1)S(1)}, u32[]{:S(2)}, u32[]{:S(2)}) collective-permute-start(bf16[8,10,1,128]{3,2,0,1:T(2,128)(2,1)S(1)} %get-tuple-element.143), channel_id=1, source_target_pairs={{0,1},{1,2},{2,3},{3,4},{4,5},{5,6},{6,7},{8,9},{9,10},{10,11},{11... | collective-permute-start | bytes 61448 | tf_op jit(solution)/shard_map/ppermute | solution.py:29
  50.0 9.6 %collective-permute-start.7 = (bf16[8,10,1,128]{3,2,0,1:T(2,128)(2,1)S(1)}, bf16[8,10,1,128]{3,2,0,1:T(2,128)(2,1)S(1)}, u32[]{:S(2)}, u32[]{:S(2)}) collective-permute-start(bf16[8,10,1,128]{3,2,0,1:T(2,128)(2,1)S(1)} %get-tuple-element.144), channel_id=1, source_target_pairs={{1,0},{2,1},{3,2},{4,3},{5,4},{6,5},{7,6},{9,8},{10,9},{11,10},{12... | collective-permute-start | bytes 61448 | tf_op jit(solution)/shard_map/ppermute | solution.py:32
  52.8 9.4 %collective-permute-start.22 = (bf16[8,10,1,128]{3,2,0,1:T(2,128)(2,1)S(1)}, bf16[8,10,1,128]{3,2,0,1:T(2,128)(2,1)S(1)}, u32[]{:S(2)}, u32[]{:S(2)}) collective-permute-start(bf16[8,10,1,128]{3,2,0,1:T(2,128)(2,1)S(1)} %get-tuple-element.151), channel_id=1, source_target_pairs={{0,1},{1,2},{2,3},{3,4},{4,5},{5,6},{6,7},{8,9},{9,10},{10,11},{11... | collective-permute-start | bytes 61448 | tf_op jit(solution)/shard_map/ppermute | solution.py:29
  65.2 12.2 %collective-permute-start.8 = (bf16[8,1,8,128]{3,2,0,1:T(8,128)(2,1)S(1)}, bf16[8,1,8,128]{3,2,0,1:T(8,128)(2,1)S(1)}, u32[]{:S(2)}, u32[]{:S(2)}) collective-permute-start(bf16[8,1,8,128]{3,2,0,1:T(8,128)(2,1)S(1)} %get-tuple-element.157), channel_id=1, source_target_pairs={{0,8},{8,16},{16,24},{24,32},{32,40},{40,48},{48,56},{56,64},{64,7... | collective-permute-start | bytes 49160 | tf_op jit(solution)/shard_map/ppermute | solution.py:29
  67.3 10.1 %collective-permute-start.9 = (bf16[8,1,8,128]{3,2,0,1:T(8,128)(2,1)S(1)}, bf16[8,1,8,128]{3,2,0,1:T(8,128)(2,1)S(1)}, u32[]{:S(2)}, u32[]{:S(2)}) collective-permute-start(bf16[8,1,8,128]{3,2,0,1:T(8,128)(2,1)S(1)} %get-tuple-element.158), channel_id=1, source_target_pairs={{8,0},{16,8},{24,16},{32,24},{40,32},{48,40},{56,48},{64,56},{72,6... | collective-permute-start | bytes 49160 | tf_op jit(solution)/shard_map/ppermute | solution.py:32
  68.7 16.2 %collective-permute-start.24 = (bf16[8,1,8,128]{3,2,0,1:T(8,128)(2,1)S(1)}, bf16[8,1,8,128]{3,2,0,1:T(8,128)(2,1)S(1)}, u32[]{:S(2)}, u32[]{:S(2)}) collective-permute-start(bf16[8,1,8,128]{3,2,0,1:T(8,128)(2,1)S(1)} %get-tuple-element.165), channel_id=1, source_target_pairs={{0,8},{8,16},{16,24},{24,32},{32,40},{40,48},{48,56},{56,64},{64,7... | collective-permute-start | bytes 49160 | tf_op jit(solution)/shard_map/ppermute | solution.py:29
  75.9 9.0 %collective-permute-start.25 = (bf16[8,1,8,128]{3,2,0,1:T(8,128)(2,1)S(1)}, bf16[8,1,8,128]{3,2,0,1:T(8,128)(2,1)S(1)}, u32[]{:S(2)}, u32[]{:S(2)}) collective-permute-start(bf16[8,1,8,128]{3,2,0,1:T(8,128)(2,1)S(1)} %get-tuple-element.166), channel_id=1, source_target_pairs={{8,0},{16,8},{24,16},{32,24},{40,32},{48,40},{56,48},{64,56},{72,6... | collective-permute-start | bytes 49160 | tf_op jit(solution)/shard_map/ppermute | solution.py:32
  77.4 15.6 %collective-permute-start.10 = (bf16[8,10,1,128]{3,2,0,1:T(2,128)(2,1)S(1)}, bf16[8,10,1,128]{3,2,0,1:T(2,128)(2,1)S(1)}, u32[]{:S(2)}, u32[]{:S(2)}) collective-permute-start(bf16[8,10,1,128]{3,2,0,1:T(2,128)(2,1)S(1)} %get-tuple-element.141), channel_id=1, source_target_pairs={{0,1},{1,2},{2,3},{3,4},{4,5},{5,6},{6,7},{8,9},{9,10},{10,11},{11... | collective-permute-start | bytes 61448 | tf_op jit(solution)/shard_map/ppermute | solution.py:29
  83.0 10.0 %collective-permute-start.11 = (bf16[8,10,1,128]{3,2,0,1:T(2,128)(2,1)S(1)}, bf16[8,10,1,128]{3,2,0,1:T(2,128)(2,1)S(1)}, u32[]{:S(2)}, u32[]{:S(2)}) collective-permute-start(bf16[8,10,1,128]{3,2,0,1:T(2,128)(2,1)S(1)} %get-tuple-element.142), channel_id=1, source_target_pairs={{1,0},{2,1},{3,2},{4,3},{5,4},{6,5},{7,6},{9,8},{10,9},{11,10},{12... | collective-permute-start | bytes 61448 | tf_op jit(solution)/shard_map/ppermute | solution.py:32
  85.0 9.6 %collective-permute-start.26 = (bf16[8,10,1,128]{3,2,0,1:T(2,128)(2,1)S(1)}, bf16[8,10,1,128]{3,2,0,1:T(2,128)(2,1)S(1)}, u32[]{:S(2)}, u32[]{:S(2)}) collective-permute-start(bf16[8,10,1,128]{3,2,0,1:T(2,128)(2,1)S(1)} %get-tuple-element.149), channel_id=1, source_target_pairs={{0,1},{1,2},{2,3},{3,4},{4,5},{5,6},{6,7},{8,9},{9,10},{10,11},{11... | collective-permute-start | bytes 61448 | tf_op jit(solution)/shard_map/ppermute | solution.py:29
  98.6 15.3 %collective-permute-start.12 = (bf16[8,1,8,128]{3,2,0,1:T(8,128)(2,1)S(1)}, bf16[8,1,8,128]{3,2,0,1:T(8,128)(2,1)S(1)}, u32[]{:S(2)}, u32[]{:S(2)}) collective-permute-start(bf16[8,1,8,128]{3,2,0,1:T(8,128)(2,1)S(1)} %get-tuple-element.155), channel_id=1, source_target_pairs={{0,8},{8,16},{16,24},{24,32},{32,40},{40,48},{48,56},{56,64},{64,7... | collective-permute-start | bytes 49160 | tf_op jit(solution)/shard_map/ppermute | solution.py:29
  102.6 11.3 %collective-permute-start.13 = (bf16[8,1,8,128]{3,2,0,1:T(8,128)(2,1)S(1)}, bf16[8,1,8,128]{3,2,0,1:T(8,128)(2,1)S(1)}, u32[]{:S(2)}, u32[]{:S(2)}) collective-permute-start(bf16[8,1,8,128]{3,2,0,1:T(8,128)(2,1)S(1)} %get-tuple-element.156), channel_id=1, source_target_pairs={{8,0},{16,8},{24,16},{32,24},{40,32},{48,40},{56,48},{64,56},{72,6... | collective-permute-start | bytes 49160 | tf_op jit(solution)/shard_map/ppermute | solution.py:32
  104.1 16.5 %collective-permute-start.28 = (bf16[8,1,8,128]{3,2,0,1:T(8,128)(2,1)S(1)}, bf16[8,1,8,128]{3,2,0,1:T(8,128)(2,1)S(1)}, u32[]{:S(2)}, u32[]{:S(2)}) collective-permute-start(bf16[8,1,8,128]{3,2,0,1:T(8,128)(2,1)S(1)} %get-tuple-element.163), channel_id=1, source_target_pairs={{0,8},{8,16},{16,24},{24,32},{32,40},{40,48},{48,56},{56,64},{64,7... | collective-permute-start | bytes 49160 | tf_op jit(solution)/shard_map/ppermute | solution.py:29
  114.0 14.7 %collective-permute-start.14 = (bf16[8,10,1,128]{3,2,0,1:T(2,128)(2,1)S(1)}, bf16[8,10,1,128]{3,2,0,1:T(2,128)(2,1)S(1)}, u32[]{:S(2)}, u32[]{:S(2)}) collective-permute-start(bf16[8,10,1,128]{3,2,0,1:T(2,128)(2,1)S(1)} %get-tuple-element.139), channel_id=1, source_target_pairs={{0,1},{1,2},{2,3},{3,4},{4,5},{5,6},{6,7},{8,9},{9,10},{10,11},{11... | collective-permute-start | bytes 61448 | tf_op jit(solution)/shard_map/ppermute | solution.py:29
  118.7 10.0 %collective-permute-start.15 = (bf16[8,10,1,128]{3,2,0,1:T(2,128)(2,1)S(1)}, bf16[8,10,1,128]{3,2,0,1:T(2,128)(2,1)S(1)}, u32[]{:S(2)}, u32[]{:S(2)}) collective-permute-start(bf16[8,10,1,128]{3,2,0,1:T(2,128)(2,1)S(1)} %get-tuple-element.140), channel_id=1, source_target_pairs={{1,0},{2,1},{3,2},{4,3},{5,4},{6,5},{7,6},{9,8},{10,9},{11,10},{12... | collective-permute-start | bytes 61448 | tf_op jit(solution)/shard_map/ppermute | solution.py:32
  120.7 9.6 %collective-permute-start.30 = (bf16[8,10,1,128]{3,2,0,1:T(2,128)(2,1)S(1)}, bf16[8,10,1,128]{3,2,0,1:T(2,128)(2,1)S(1)}, u32[]{:S(2)}, u32[]{:S(2)}) collective-permute-start(bf16[8,10,1,128]{3,2,0,1:T(2,128)(2,1)S(1)} %get-tuple-element.147), channel_id=1, source_target_pairs={{0,1},{1,2},{2,3},{3,4},{4,5},{5,6},{6,7},{8,9},{9,10},{10,11},{11... | collective-permute-start | bytes 61448 | tf_op jit(solution)/shard_map/ppermute | solution.py:29
  134.3 15.5 %collective-permute-start.16 = (bf16[8,1,8,128]{3,2,0,1:T(8,128)(2,1)S(1)}, bf16[8,1,8,128]{3,2,0,1:T(8,128)(2,1)S(1)}, u32[]{:S(2)}, u32[]{:S(2)}) collective-permute-start(bf16[8,1,8,128]{3,2,0,1:T(8,128)(2,1)S(1)} %get-tuple-element.153), channel_id=1, source_target_pairs={{0,8},{8,16},{16,24},{24,32},{32,40},{40,48},{48,56},{56,64},{64,7... | collective-permute-start | bytes 49160 | tf_op jit(solution)/shard_map/ppermute | solution.py:29
  138.9 10.9 %collective-permute-start.17 = (bf16[8,1,8,128]{3,2,0,1:T(8,128)(2,1)S(1)}, bf16[8,1,8,128]{3,2,0,1:T(8,128)(2,1)S(1)}, u32[]{:S(2)}, u32[]{:S(2)}) collective-permute-start(bf16[8,1,8,128]{3,2,0,1:T(8,128)(2,1)S(1)} %get-tuple-element.154), channel_id=1, source_target_pairs={{8,0},{16,8},{24,16},{32,24},{40,32},{48,40},{56,48},{64,56},{72,6... | collective-permute-start | bytes 49160 | tf_op jit(solution)/shard_map/ppermute | solution.py:32
  140.4 15.5 %collective-permute-start.32 = (bf16[8,1,8,128]{3,2,0,1:T(8,128)(2,1)S(1)}, bf16[8,1,8,128]{3,2,0,1:T(8,128)(2,1)S(1)}, u32[]{:S(2)}, u32[]{:S(2)}) collective-permute-start(bf16[8,1,8,128]{3,2,0,1:T(8,128)(2,1)S(1)} %get-tuple-element.161), channel_id=1, source_target_pairs={{0,8},{8,16},{16,24},{24,32},{32,40},{40,48},{48,56},{56,64},{64,7... | collective-permute-start | bytes 49160 | tf_op jit(solution)/shard_map/ppermute | solution.py:29
  149.9 14.0 %collective-permute-start.18 = (bf16[8,10,1,128]{3,2,0,1:T(2,128)(2,1)S(1)}, bf16[8,10,1,128]{3,2,0,1:T(2,128)(2,1)S(1)}, u32[]{:S(2)}, u32[]{:S(2)}) collective-permute-start(bf16[8,10,1,128]{3,2,0,1:T(2,128)(2,1)S(1)} %get-tuple-element.137), channel_id=1, source_target_pairs={{0,1},{1,2},{2,3},{3,4},{4,5},{5,6},{6,7},{8,9},{9,10},{10,11},{11... | collective-permute-start | bytes 61448 | tf_op jit(solution)/shard_map/ppermute | solution.py:29
  153.9 10.0 %collective-permute-start.19 = (bf16[8,10,1,128]{3,2,0,1:T(2,128)(2,1)S(1)}, bf16[8,10,1,128]{3,2,0,1:T(2,128)(2,1)S(1)}, u32[]{:S(2)}, u32[]{:S(2)}) collective-permute-start(bf16[8,10,1,128]{3,2,0,1:T(2,128)(2,1)S(1)} %get-tuple-element.138), channel_id=1, source_target_pairs={{1,0},{2,1},{3,2},{4,3},{5,4},{6,5},{7,6},{9,8},{10,9},{11,10},{12... | collective-permute-start | bytes 61448 | tf_op jit(solution)/shard_map/ppermute | solution.py:32
  155.9 17.8 %collective-permute-start.34 = (bf16[8,10,1,128]{3,2,0,1:T(2,128)(2,1)S(1)}, bf16[8,10,1,128]{3,2,0,1:T(2,128)(2,1)S(1)}, u32[]{:S(2)}, u32[]{:S(2)}) collective-permute-start(bf16[8,10,1,128]{3,2,0,1:T(2,128)(2,1)S(1)} %get-tuple-element.145), channel_id=1, source_target_pairs={{0,1},{1,2},{2,3},{3,4},{4,5},{5,6},{6,7},{8,9},{9,10},{10,11},{11... | collective-permute-start | bytes 61448 | tf_op jit(solution)/shard_map/ppermute | solution.py:29
  162.0 11.7 %collective-permute-start.35 = (bf16[8,10,1,128]{3,2,0,1:T(2,128)(2,1)S(1)}, bf16[8,10,1,128]{3,2,0,1:T(2,128)(2,1)S(1)}, u32[]{:S(2)}, u32[]{:S(2)}) collective-permute-start(bf16[8,10,1,128]{3,2,0,1:T(2,128)(2,1)S(1)} %get-tuple-element.146), channel_id=1, source_target_pairs={{1,0},{2,1},{3,2},{4,3},{5,4},{6,5},{7,6},{9,8},{10,9},{11,10},{12... | collective-permute-start | bytes 61448 | tf_op jit(solution)/shard_map/ppermute | solution.py:32
  166.1 15.6 %all-to-all-start = ((bf16[32,8,8,128]{3,2,0,1:T(8,128)(2,1)}), bf16[32,8,8,128]{3,2,0,1:T(8,128)(2,1)S(1)}, u32[]{:S(2)}, u32[]{:S(2)}) async-start(bf16[32,8,8,128]{3,2,0,1:T(8,128)(2,1)} %pad_maximum_fusion.1), calls=%async_computation | async-start | bytes 1048576 | tf_op jit(solution)/shard_map/all_to_all | solution.py:175
  181.7 14.4 %all-to-all-start.1 = ((bf16[32,8,8,128]{3,2,0,1:T(8,128)(2,1)}), bf16[32,8,8,128]{3,2,0,1:T(8,128)(2,1)S(1)}, u32[]{:S(2)}, u32[]{:S(2)}) async-start(bf16[32,8,8,128]{3,2,0,1:T(8,128)(2,1)} %pad_maximum_fusion.2), calls=%async_computation.1 | async-start | bytes 1048576 | tf_op jit(solution)/shard_map/all_to_all | solution.py:175
  187.7 100.1 %all-reduce.24.cloned.1.call-start = ((), (), s32[]{:S(2)}) async-start(), calls=%async_computation.2 | async-start | bytes 983040 | tf_op jit(solution)/shard_map/psum | solution.py:17
  199.9 374.8 %all-reduce.26.cloned.1.call-start = ((), (), s32[]{:S(2)}) async-start(), calls=%async_computation.3 | async-start | bytes 983040 | tf_op jit(solution)/shard_map/psum | solution.py:17
  (18 other events, 269.4 us)
Sparse Core Ops, SparseCore 0:
  200.0 87.6 all-reduce.23
  290.4 284.3 all-reduce.25
